TPU v7x, 512 devices: a whole 4x4x16 slice. The times are simulated.
512 devices in a mesh: gx: 16 (over z_hi, y, core), gy: 4 (over x), gz: 8 (over z_lo).
Axes of the slice: x: 4, y: 4, z: 16 (z_hi: 2, z_lo: 8; z = z_hi * 8 + z_lo), core: 2. Of those that a mesh axis runs over, the one named last changes fastest.
Arguments:
- body_load: float32 [32, 16, 64, 192], P('gx', 'gy', 'gz'), may hold values from -6 to 6
- probe_load: float32 [32, 16, 64, 192], P('gx', 'gy', 'gz'), may hold values from -6 to 6
- density: float32 [32, 16, 64], P('gx', 'gy', 'gz'), may hold values from 0.3 to 1
- link_types: int32 [32, 16, 64, 7], P('gx', 'gy', 'gz'), may hold values from 0 to 4, as said below
- off_blocks: bfloat16 [4, 192, 192], replicated, may hold values from -0.4375 to 0.4375
- self_blocks: bfloat16 [4, 192, 192], replicated, as said below
- block_owner: int32 [32, 16, 64], P('gx', 'gy', 'gz'), may hold values from 0 to 4095, as said below
Outputs:
- state_field: float32 [32, 16, 64, 192], P('gx', 'gy', 'gz')
- adjoint_field: float32 [32, 16, 64, 192], P('gx', 'gy', 'gz')
- coarse_sensitivity: float32 [4096], P(('gx', 'gy', 'gz'))
Inputs may be any that keep to these rules, and one draw needn't show every extreme that they name: `link_types`: entries 0, 1, 2 of a group name the kind of its coupling to the next group along the first, second and third dimension (4: no coupling, always so on the grid's last layer); entry 3 + k equals entry k of the group one step lower along dimension k (4 on the first layer); entry 6 names the kind of the group's own block and is below 4. `block_owner`: every design block is named by exactly 8 node groups. `self_blocks`: each own block is symmetric and its diagonal entries exceed 3.8.
All inputs are finite; a program needn't handle non-finite values.
Results may differ from a plain program's by a relative error of at most 0.0012.
Values may be sent and summed in bfloat16 or wider, within the bound.
A program may use at most 64 MiB of HBM per device.

v0:
```python
import jax
import jax.numpy as jnp
from jax import lax
from jax.sharding import PartitionSpec as P

ITERS = 4
GPB = 8


def with_halo(array, sides, width):
    for axis, dim in sides:
        peers, length = (lax.axis_size(axis), array.shape[dim])
        up = [(i, (i + 1) % peers) for i in range(peers - 1)]
        down = [(j, i) for i, j in up]
        last = lax.slice_in_dim(array, length - width, length, axis=dim)
        initial = lax.slice_in_dim(array, 0, width, axis=dim)
        before = lax.ppermute(last, axis, up)
        after = lax.ppermute(initial, axis, down)
        array = jnp.concatenate([before, array, after], axis=dim)
    return array


def level_masks(type_codes, level_count):
    levels = lax.broadcasted_iota(jnp.int32, type_codes.shape + (level_count,), 3)
    return (type_codes[..., None] == levels).astype(jnp.bfloat16)


def typed_product(window, selector, block_table):
    spread = window[:, :, :, :, None, :] * selector[None, :, :, :, :, None]
    flattened = spread.reshape(-1, block_table.shape[0])
    return jnp.dot(flattened, block_table, preferred_element_type=jnp.float32).reshape(window.shape)


def cut_window(padded, shift):
    span_x = padded.shape[1] - 2
    span_y = padded.shape[2] - 2
    span_z = padded.shape[3] - 2
    return padded[
        :,
        1 + shift[0] : 1 + shift[0] + span_x,
        1 + shift[1] : 1 + shift[1] + span_y,
        1 + shift[2] : 1 + shift[2] + span_z,
        :,
    ]


def local_image(padded, selectors, tables, stiff_scale):
    up_table, low_table, own_table = tables
    accumulated = typed_product(cut_window(padded, (0, 0, 0)), selectors[6], own_table)
    offsets = ((1, 0, 0), (0, 1, 0), (0, 0, 1))
    for k in range(3):
        upper = offsets[k]
        lower = (-upper[0], -upper[1], -upper[2])
        accumulated = accumulated + typed_product(cut_window(padded, upper), selectors[k], up_table)
        accumulated = accumulated + typed_product(
            cut_window(padded, lower), selectors[3 + k], low_table
        )
    return accumulated * stiff_scale[None, :, :, :, None]


def local(body_load, probe_load, density, link_types, off_blocks, self_blocks, block_owner):
    dof_count = body_load.shape[-1]
    type_count = off_blocks.shape[0]
    self_count = self_blocks.shape[0]
    stiff_scale = density**1.5
    selectors = [level_masks(link_types[..., j], type_count) for j in range(6)]
    selectors.append(level_masks(link_types[..., 6], self_count))
    up_table = jnp.swapaxes(off_blocks, 1, 2).reshape(type_count * dof_count, dof_count)
    low_table = off_blocks.reshape(type_count * dof_count, dof_count)
    own_table = self_blocks.reshape(self_count * dof_count, dof_count)
    tables = (up_table, low_table, own_table)
    diagonals = jnp.diagonal(self_blocks, axis1=1, axis2=2).astype(jnp.float32)
    pivots = jnp.zeros(body_load.shape, jnp.float32)
    for level in range(self_count):
        pivots = (
            pivots + selectors[6][..., level : level + 1].astype(jnp.float32) * diagonals[level]
        )
    targets = jnp.stack([body_load, probe_load])
    residual = targets
    solution = jnp.zeros_like(targets)
    for sweep in range(ITERS):
        precond = residual / pivots[None]
        shipped = (precond * stiff_scale[None, :, :, :, None]).astype(jnp.bfloat16)
        padded = with_halo(shipped, (("gx", 1), ("gy", 2), ("gz", 3)), 1)
        image_field = local_image(padded, selectors, tables, stiff_scale)
        projected = jnp.sum(residual * image_field, axis=(1, 2, 3, 4))
        energy = jnp.sum(image_field * image_field, axis=(1, 2, 3, 4))
        projected, energy = lax.psum((projected, energy), ("gx", "gy", "gz"))
        step_size = projected / (energy + 1e-06)
        solution = solution + step_size[:, None, None, None, None] * precond
        residual = residual - step_size[:, None, None, None, None] * image_field
    applied = targets - residual
    bracket = jnp.sum(solution[1] * applied[0] + solution[0] * applied[1], axis=-1)
    sensitivity = -1.5 * bracket / density
    weighted = density * sensitivity
    groups_here = density.shape[0] * density.shape[1] * density.shape[2]
    blocks_here = groups_here // GPB
    size_x = lax.axis_size("gx")
    size_y = lax.axis_size("gy")
    size_z = lax.axis_size("gz")
    block_total = blocks_here * size_x * size_y * size_z
    owners = block_owner.reshape(-1)
    numerator = jnp.zeros((block_total,), jnp.float32).at[owners].add(weighted.reshape(-1))
    denominator = jnp.zeros((block_total,), jnp.float32).at[owners].add(density.reshape(-1))
    numerator, denominator = (
        lax.psum_scatter(numerator, ("gx", "gy", "gz"), scatter_dimension=0, tiled=True),
        lax.psum_scatter(denominator, ("gx", "gy", "gz"), scatter_dimension=0, tiled=True),
    )
    return (solution[0], solution[1], numerator / denominator)


def solution(mesh):
    in_specs = (
        P("gx", "gy", "gz", None),
        P("gx", "gy", "gz", None),
        P("gx", "gy", "gz"),
        P("gx", "gy", "gz", None),
        P(),
        P(),
        P("gx", "gy", "gz"),
    )
    out_specs = (P("gx", "gy", "gz", None), P("gx", "gy", "gz", None), P(("gx", "gy", "gz")))
    return jax.shard_map(local, mesh=mesh, in_specs=in_specs, out_specs=out_specs, check_vma=False)
```

profile of v0, /device:TPU:1, one launch (start us, length us, event | category | flops | bytes accessed | tf_op | source)
XLA Modules:
  0.0 689.2 jit_solution(9838900810073035173)
XLA Ops:
  1.5 7.8 %copy.38 = bf16[4,192,192]{0,2,1:T(8,128)(2,1)} copy(bf16[4,192,192]{2,1,0:T(8,128)(2,1)} %param.12) | data formatting | bytes 589824 | tf_op args[5]
  9.3 5.3 gather_fusion
  15.2 8.8 %collective-permute-start = (bf16[2,1,4,8,192]{4,3,2,1,0:T(8,128)(2,1)S(1)}, bf16[2,1,4,8,192]{4,3,2,1,0:T(8,128)(2,1)S(1)}, u32[]{:S(2)}, u32[]{:S(2)}) collective-permute-start(bf16[2,1,4,8,192]{4,3,2,1,0:T(8,128)(2,1)S(1)} %get-tuple-element.83), channel_id=1, source_target_pairs={{32,0},{64,32},{96,64},{128,96},{160,128},{192,160},{224,192},{256... | collective-permute-start | bytes 73736 | tf_op jit(solution)/shard_map/ppermute | solution.py:18
  24.0 1.9 collective-permute-start.1
  28.5 4.0 collective-permute-start.3
  34.8 4.0 collective-permute-start.5
  41.4 125.0 %all-reduce.6 = (f32[2]{0:T(128)S(1)}, f32[2]{0:T(128)S(1)}) all-reduce(f32[2]{0:T(128)S(1)} %get-tuple-element.10, f32[2]{0:T(128)S(1)} %get-tuple-element.9), channel_id=1, replica_groups=mesh['gx'=16,'gy'=4,'gz'=8] {'gx','gy','gz'}, use_global_device_ids=true, to_apply=%region_1.2 | all-reduce | flops 4 | bytes 32 | tf_op jit(solution)/shard_map/psum | solution.py:88
  166.6 2.9 collective-permute-start.6
  169.5 2.7 collective-permute-start.7
  174.5 4.0 collective-permute-start.9
  180.9 4.0 collective-permute-start.11
  187.5 117.6 %all-reduce.5 = (f32[2]{0:T(128)S(1)}, f32[2]{0:T(128)S(1)}) all-reduce(f32[2]{0:T(128)S(1)} %get-tuple-element.8, f32[2]{0:T(128)S(1)} %get-tuple-element.7), channel_id=1, replica_groups=mesh['gx'=16,'gy'=4,'gz'=8] {'gx','gy','gz'}, use_global_device_ids=true, to_apply=%region_5.6 | all-reduce | flops 4 | bytes 32 | tf_op jit(solution)/shard_map/psum | solution.py:88
  305.2 2.6 collective-permute-start.12
  307.8 3.0 collective-permute-start.13
  311.8 1.3 collective-permute-start.14
  313.1 4.0 collective-permute-start.15
  319.6 4.0 collective-permute-start.17
  326.2 120.1 %all-reduce.4 = (f32[2]{0:T(128)S(1)}, f32[2]{0:T(128)S(1)}) all-reduce(f32[2]{0:T(128)S(1)} %get-tuple-element.6, f32[2]{0:T(128)S(1)} %get-tuple-element.5), channel_id=1, replica_groups=mesh['gx'=16,'gy'=4,'gz'=8] {'gx','gy','gz'}, use_global_device_ids=true, to_apply=%region_9.10 | all-reduce | flops 4 | bytes 32 | tf_op jit(solution)/shard_map/psum | solution.py:88
  446.4 3.1 collective-permute-start.18
  449.6 2.5 collective-permute-start.19
  454.6 4.0 collective-permute-start.21
  461.0 4.0 collective-permute-start.23
  467.6 118.0 %all-reduce.3 = (f32[2]{0:T(128)S(1)}, f32[2]{0:T(128)S(1)}) all-reduce(f32[2]{0:T(128)S(1)} %get-tuple-element.4, f32[2]{0:T(128)S(1)} %get-tuple-element.3), channel_id=1, replica_groups=mesh['gx'=16,'gy'=4,'gz'=8] {'gx','gy','gz'}, use_global_device_ids=true, to_apply=%region_13.14 | all-reduce | flops 4 | bytes 32 | tf_op jit(solution)/shard_map/psum | solution.py:88
  587.4 101.2 %all-reduce.2 = (f32[4096]{0:T(1024)S(1)}, f32[4096]{0:T(1024)S(1)}) all-reduce(f32[4096]{0:T(1024)S(1)} %scatter_custom_fusion.1, f32[4096]{0:T(1024)S(1)} %scatter_custom_fusion), channel_id=3, replica_groups=mesh['gx'=16,'gy'=4,'gz'=8] {'gx','gy','gz'}, use_global_device_ids=true, to_apply=%region_20.21.clone | all-reduce | flops 8192 | bytes 65536
  (123 shorter events, 32.1 us)
Async XLA Ops:
  15.2 10.8 %collective-permute-start = (bf16[2,1,4,8,192]{4,3,2,1,0:T(8,128)(2,1)S(1)}, bf16[2,1,4,8,192]{4,3,2,1,0:T(8,128)(2,1)S(1)}, u32[]{:S(2)}, u32[]{:S(2)}) collective-permute-start(bf16[2,1,4,8,192]{4,3,2,1,0:T(8,128)(2,1)S(1)} %get-tuple-element.83), channel_id=1, source_target_pairs={{32,0},{64,32},{96,64},{128,96},{160,128},{192,160},{224,192},{256... | collective-permute-start | bytes 73736 | tf_op jit(solution)/shard_map/ppermute | solution.py:18
  24.0 3.1 collective-permute-start.1
  27.2 5.6 collective-permute-start.2
  28.5 5.0 collective-permute-start.3
  33.5 6.0 collective-permute-start.4
  34.8 5.2 collective-permute-start.5
  166.6 5.6 collective-permute-start.6
  169.5 3.7 collective-permute-start.7
  173.2 5.6 collective-permute-start.8
  174.5 5.0 collective-permute-start.9
  179.6 6.0 collective-permute-start.10
  180.9 5.2 collective-permute-start.11
  305.2 5.7 collective-permute-start.12
  307.8 4.0 collective-permute-start.13
  311.8 5.6 collective-permute-start.14
  313.1 5.2 collective-permute-start.15
  318.3 6.0 collective-permute-start.16
  319.6 5.2 collective-permute-start.17
  446.4 6.8 collective-permute-start.18
  449.6 3.7 collective-permute-start.19
  453.3 5.6 collective-permute-start.20
  454.6 5.0 collective-permute-start.21
  459.7 6.0 collective-permute-start.22
  461.0 5.2 collective-permute-start.23
  (7 other events, 651.9 us)
where the time goes:
time: 691 us; the launch traced here: 689 us
  blocking collectives  582 us (84%)
  starting transfers between devices  69.6 us (10%)
  local copies, waits for them, and re-layouts  14.6 us (2%)
  matrix products  9.27 us (1%)
  waiting for transfers between devices  7.56 us (1%)
    psum x4, blocking collectives, local(): projected, energy = lax.psum((projected, energy), ('gx', 'gy', 'gz'))  481 us
    unnamed x1, blocking collectives  101 us
    ppermute x12, starting transfers between devices, with_halo(): before = lax.ppermute(last, axis, up)  41.9 us
    ppermute x12, starting transfers between devices, with_halo(): after = lax.ppermute(initial, axis, down)  27.7 us
  transfers between devices with their start and end apart: 24, of which 11 were waited for; matrix products, arithmetic and copies ran while one was open for 1% of the time, Pallas kernels for 0%

commit v1 on v0

--- a/solution.py
+++ b/solution.py
@@ -5,6 +5,11 @@
 
 ITERS = 4
 GPB = 8
+
+
+def axis_by_axis(array_2, first, second):
+    half = lax.psum(array_2, first)
+    return lax.psum(half, second)
 
 
 def with_halo(array, sides, width):
@@ -85,7 +90,7 @@
         image_field = local_image(padded, selectors, tables, stiff_scale)
         projected = jnp.sum(residual * image_field, axis=(1, 2, 3, 4))
         energy = jnp.sum(image_field * image_field, axis=(1, 2, 3, 4))
-        projected, energy = lax.psum((projected, energy), ("gx", "gy", "gz"))
+        projected, energy = axis_by_axis((projected, energy), ("gy", "gz"), "gx")
         step_size = projected / (energy + 1e-06)
         solution = solution + step_size[:, None, None, None, None] * precond
         residual = residual - step_size[:, None, None, None, None] * image_field

time: 691 us -> 985 us (1.43)
  blocking collectives: 582 us -> 867 us
    psum x4 -> x8, blocking collectives: 481 us -> 730 us  [the longest x4 414 us: axis_by_axis(): half = lax.psum(array_2, first)]
    unnamed x1, blocking collectives: 101 us -> 137 us
    ppermute x12, starting transfers between devices: 41.9 us -> 52.9 us  [with_halo(): before = lax.ppermute(last, axis, up)]
where the time goes in v1:
time: 985 us; the launch traced here: 983 us
  blocking collectives  867 us (88%)
  starting transfers between devices  79.2 us (8%)
  local copies, waits for them, and re-layouts  14.6 us (1%)
    psum x4, blocking collectives, axis_by_axis(): half = lax.psum(array_2, first)  414 us
    psum x4, blocking collectives, axis_by_axis(): return lax.psum(half, second)  316 us
    unnamed x1, blocking collectives  137 us
    ppermute x12, starting transfers between devices, with_halo(): before = lax.ppermute(last, axis, up)  52.9 us
    ppermute x12, starting transfers between devices, with_halo(): after = lax.ppermute(initial, axis, down)  26.3 us
  transfers between devices with their start and end apart: 24, of which 11 were waited for; matrix products, arithmetic and copies ran while one was open for 1% of the time, Pallas kernels for 0%

profile of v1, /device:TPU:1, one launch (start us, length us, event | category | flops | bytes accessed | tf_op | source)
XLA Modules:
  0.0 983.5 jit_solution(1623971702019658521)
XLA Ops:
  1.5 7.8 copy.38
  9.3 5.4 gather_fusion
  15.3 8.8 collective-permute-start
  28.5 4.0 collective-permute-start.3
  34.9 4.0 collective-permute-start.5
  41.5 109.4 %all-reduce.6 = (f32[2]{0:T(128)S(1)}, f32[2]{0:T(128)S(1)}) all-reduce(f32[2]{0:T(128)S(1)} %get-tuple-element.10, f32[2]{0:T(128)S(1)} %get-tuple-element.9), channel_id=1, replica_groups=mesh['gx'=16,'gy'=4,'gz'=8] {'gy','gz'}, use_global_device_ids=true, to_apply=%region_1.2 | all-reduce | flops 4 | bytes 32 | tf_op jit(solution)/shard_map/psum | solution.py:11
  150.9 77.4 %all-reduce.10 = (f32[2]{0:T(128)S(1)}, f32[2]{0:T(128)S(1)}) all-reduce(f32[2]{0:T(128)S(1)} %get-tuple-element.23, f32[2]{0:T(128)S(1)} %get-tuple-element.24), channel_id=1, replica_groups=mesh['gx'=16,'gy'=4,'gz'=8] {'gx'}, use_global_device_ids=true, to_apply=%region_2.3 | all-reduce | flops 4 | bytes 32 | tf_op jit(solution)/shard_map/psum | solution.py:12
  228.4 2.6 collective-permute-start.6
  230.9 3.0 collective-permute-start.7
  236.3 4.0 collective-permute-start.9
  242.8 4.0 collective-permute-start.11
  249.5 101.3 %all-reduce.5 = (f32[2]{0:T(128)S(1)}, f32[2]{0:T(128)S(1)}) all-reduce(f32[2]{0:T(128)S(1)} %get-tuple-element.8, f32[2]{0:T(128)S(1)} %get-tuple-element.7), channel_id=1, replica_groups=mesh['gx'=16,'gy'=4,'gz'=8] {'gy','gz'}, use_global_device_ids=true, to_apply=%region_7.8 | all-reduce | flops 4 | bytes 32 | tf_op jit(solution)/shard_map/psum | solution.py:11
  350.8 77.0 %all-reduce.9 = (f32[2]{0:T(128)S(1)}, f32[2]{0:T(128)S(1)}) all-reduce(f32[2]{0:T(128)S(1)} %get-tuple-element.21, f32[2]{0:T(128)S(1)} %get-tuple-element.22), channel_id=1, replica_groups=mesh['gx'=16,'gy'=4,'gz'=8] {'gx'}, use_global_device_ids=true, to_apply=%region_8.9 | all-reduce | flops 4 | bytes 32 | tf_op jit(solution)/shard_map/psum | solution.py:12
  430.4 3.9 collective-permute-start.13
  436.6 4.0 collective-permute-start.15
  443.0 4.0 collective-permute-start.17
  449.7 101.4 %all-reduce.4 = (f32[2]{0:T(128)S(1)}, f32[2]{0:T(128)S(1)}) all-reduce(f32[2]{0:T(128)S(1)} %get-tuple-element.6, f32[2]{0:T(128)S(1)} %get-tuple-element.5), channel_id=1, replica_groups=mesh['gx'=16,'gy'=4,'gz'=8] {'gy','gz'}, use_global_device_ids=true, to_apply=%region_13.14 | all-reduce | flops 4 | bytes 32 | tf_op jit(solution)/shard_map/psum | solution.py:11
  551.1 80.9 %all-reduce.8 = (f32[2]{0:T(128)S(1)}, f32[2]{0:T(128)S(1)}) all-reduce(f32[2]{0:T(128)S(1)} %get-tuple-element.19, f32[2]{0:T(128)S(1)} %get-tuple-element.20), channel_id=1, replica_groups=mesh['gx'=16,'gy'=4,'gz'=8] {'gx'}, use_global_device_ids=true, to_apply=%region_14.15 | all-reduce | flops 4 | bytes 32 | tf_op jit(solution)/shard_map/psum | solution.py:12
  634.2 12.2 %collective-permute-start.19 = (bf16[2,1,4,8,192]{4,3,2,1,0:T(8,128)(2,1)S(1)}, bf16[2,1,4,8,192]{4,3,2,1,0:T(8,128)(2,1)S(1)}, u32[]{:S(2)}, u32[]{:S(2)}) collective-permute-start(bf16[2,1,4,8,192]{4,3,2,1,0:T(8,128)(2,1)S(1)} %get-tuple-element.84), channel_id=1, source_target_pairs={{0,32},{32,64},{64,96},{96,128},{128,160},{160,192},{192,224},{224... | collective-permute-start | bytes 73736 | tf_op jit(solution)/shard_map/ppermute | solution.py:22
  648.8 4.0 collective-permute-start.21
  655.2 4.0 collective-permute-start.23
  661.8 101.8 %all-reduce.3 = (f32[2]{0:T(128)S(1)}, f32[2]{0:T(128)S(1)}) all-reduce(f32[2]{0:T(128)S(1)} %get-tuple-element.4, f32[2]{0:T(128)S(1)} %get-tuple-element.3), channel_id=1, replica_groups=mesh['gx'=16,'gy'=4,'gz'=8] {'gy','gz'}, use_global_device_ids=true, to_apply=%region_19.20 | all-reduce | flops 4 | bytes 32 | tf_op jit(solution)/shard_map/psum | solution.py:11
  763.6 80.6 %all-reduce.7 = (f32[2]{0:T(128)S(1)}, f32[2]{0:T(128)S(1)}) all-reduce(f32[2]{0:T(128)S(1)} %get-tuple-element.17, f32[2]{0:T(128)S(1)} %get-tuple-element.18), channel_id=1, replica_groups=mesh['gx'=16,'gy'=4,'gz'=8] {'gx'}, use_global_device_ids=true, to_apply=%region_20.21 | all-reduce | flops 4 | bytes 32 | tf_op jit(solution)/shard_map/psum | solution.py:12
  846.0 136.9 %all-reduce.2 = (f32[4096]{0:T(1024)S(1)}, f32[4096]{0:T(1024)S(1)}) all-reduce(f32[4096]{0:T(1024)S(1)} %scatter_custom_fusion.1, f32[4096]{0:T(1024)S(1)} %scatter_custom_fusion), channel_id=3, replica_groups=mesh['gx'=16,'gy'=4,'gz'=8] {'gx','gy','gz'}, use_global_device_ids=true, to_apply=%region_28.29.clone | all-reduce | flops 8192 | bytes 65536
  (127 shorter events, 39.9 us)
Async XLA Ops:
  15.3 10.8 %collective-permute-start = (bf16[2,1,4,8,192]{4,3,2,1,0:T(8,128)(2,1)S(1)}, bf16[2,1,4,8,192]{4,3,2,1,0:T(8,128)(2,1)S(1)}, u32[]{:S(2)}, u32[]{:S(2)}) collective-permute-start(bf16[2,1,4,8,192]{4,3,2,1,0:T(8,128)(2,1)S(1)} %get-tuple-element.91), channel_id=1, source_target_pairs={{32,0},{64,32},{96,64},{128,96},{160,128},{192,160},{224,192},{256... | collective-permute-start | bytes 73736 | tf_op jit(solution)/shard_map/ppermute | solution.py:23
  24.1 3.1 collective-permute-start.1
  27.2 5.6 collective-permute-start.2
  28.5 5.0 collective-permute-start.3
  33.6 6.0 collective-permute-start.4
  34.9 5.2 collective-permute-start.5
  228.4 5.6 collective-permute-start.6
  230.9 4.0 collective-permute-start.7
  235.0 5.6 collective-permute-start.8
  236.3 5.2 collective-permute-start.9
  241.5 6.0 collective-permute-start.10
  242.8 5.2 collective-permute-start.11
  427.9 6.5 collective-permute-start.12
  430.4 4.9 collective-permute-start.13
  435.3 5.6 collective-permute-start.14
  436.6 5.0 collective-permute-start.15
  441.7 6.0 collective-permute-start.16
  443.0 5.3 collective-permute-start.17
  632.1 15.4 %collective-permute-start.18 = (bf16[2,1,4,8,192]{4,3,2,1,0:T(8,128)(2,1)S(1)}, bf16[2,1,4,8,192]{4,3,2,1,0:T(8,128)(2,1)S(1)}, u32[]{:S(2)}, u32[]{:S(2)}) collective-permute-start(bf16[2,1,4,8,192]{4,3,2,1,0:T(8,128)(2,1)S(1)} %get-tuple-element.85), channel_id=1, source_target_pairs={{32,0},{64,32},{96,64},{128,96},{160,128},{192,160},{224,192},{256... | collective-permute-start | bytes 73736 | tf_op jit(solution)/shard_map/ppermute | solution.py:23
  634.2 13.3 %collective-permute-start.19 = (bf16[2,1,4,8,192]{4,3,2,1,0:T(8,128)(2,1)S(1)}, bf16[2,1,4,8,192]{4,3,2,1,0:T(8,128)(2,1)S(1)}, u32[]{:S(2)}, u32[]{:S(2)}) collective-permute-start(bf16[2,1,4,8,192]{4,3,2,1,0:T(8,128)(2,1)S(1)} %get-tuple-element.84), channel_id=1, source_target_pairs={{0,32},{32,64},{64,96},{96,128},{128,160},{160,192},{192,224},{224... | collective-permute-start | bytes 73736 | tf_op jit(solution)/shard_map/ppermute | solution.py:22
  647.5 5.6 collective-permute-start.20
  648.8 5.0 collective-permute-start.21
  653.9 6.0 collective-permute-start.22
  655.2 5.2 collective-permute-start.23
  (7 other events, 908.2 us)
